TPU v7x, 256 devices: a whole 4x4x8 slice. The times are simulated.
256 devices in a mesh: rows: 16 (over y, x), keys: 16 (over z, core).
Axes of the slice: x: 4, y: 4, z: 8, core: 2. Of those that a mesh axis runs over, the one named last changes fastest.
Arguments:
- pair_rep: bfloat16 [768, 768, 128], P('rows', 'keys'), may hold values from -6 to 6
- norm_gain: float32 [128], replicated, may hold values from 0.1 to 1.9
- w_query: bfloat16 [128, 128], replicated, may hold values from -0.5 to 0.5
- w_key: bfloat16 [128, 128], replicated, may hold values from -0.5 to 0.5
- w_value: bfloat16 [128, 128], replicated, may hold values from -0.5 to 0.5
- w_gate: bfloat16 [128, 128], replicated, may hold values from -0.5 to 0.5
- w_out: bfloat16 [128, 128], replicated, may hold values from -0.5 to 0.5
- pair_bias: bfloat16 [4, 768, 768], P(None, 'keys', 'rows'), may hold values from -12 to 300
Outputs:
- update: bfloat16 [768, 768, 128], P('rows', 'keys')
All inputs are finite; a program needn't handle non-finite values.
Results may differ from a plain program's by a relative error of at most 0.025.
Values may be sent and summed in bfloat16 or wider, within the bound.
A program may use at most 128 MiB of HBM per device.

v0:
```python
import jax
import jax.numpy as jnp
from jax import lax
from jax.sharding import Mesh
from jax.sharding import PartitionSpec as P

ROWS = ("rows_0", "rows_1")
epsilon = 1e-05
block_rows = 8


def gathered_by_axis(array, axes, dim):
    out = array
    for number in range(len(axes) - 1, -1, -1):
        out = lax.all_gather(out, axes[number], axis=dim, tiled=True)
    return out


def normalize(pair_rep, norm_gain):
    values = pair_rep.astype(jnp.float32)
    center = jnp.mean(values, axis=-1, keepdims=True)
    spread = jnp.mean(jnp.square(values - center), axis=-1, keepdims=True)
    return ((values - center) * lax.rsqrt(spread + epsilon) * norm_gain).astype(jnp.bfloat16)


def split_heads(tensor, head_count):
    return tensor.reshape(tensor.shape[:-1] + (head_count, tensor.shape[-1] // head_count))


def blocked(tensor):
    return tensor.reshape((tensor.shape[0] // block_rows, block_rows) + tensor.shape[1:])


def unblocked(tensor):
    return tensor.reshape((tensor.shape[0] * tensor.shape[1],) + tensor.shape[2:])


def absorb(running, query_block, key_block, value_block, bias_piece, head_count):
    highest, totals, summed = running
    logits = (
        jnp.einsum(
            "rjhd,rkhd->rhjk",
            split_heads(query_block, head_count),
            split_heads(key_block, head_count),
            preferred_element_type=jnp.float32,
        )
        + bias_piece.astype(jnp.float32)[None]
    )
    new_highest = jnp.maximum(highest, jnp.max(logits, axis=3))
    shrink = jnp.exp(highest - new_highest)
    powers = jnp.exp(logits - new_highest[..., None])
    totals = totals * shrink + jnp.sum(powers, axis=3)
    summed = summed * jnp.transpose(shrink, (0, 2, 1))[..., None] + jnp.einsum(
        "rhjk,rkhd->rjhd",
        powers.astype(jnp.bfloat16),
        split_heads(value_block, head_count),
        preferred_element_type=jnp.float32,
    )
    return (new_highest, totals, summed)


def body(pair_rep, norm_gain, w_query, w_key, w_value, w_gate, w_out, pair_bias):
    head_count = pair_bias.shape[0]
    inner_width = w_query.shape[1]
    normed = normalize(pair_rep, norm_gain)
    local_rows, local_keys = (normed.shape[0], normed.shape[1])
    queries = (
        jnp.dot(normed, w_query, preferred_element_type=jnp.float32)
        * (inner_width // head_count) ** (-0.5)
    ).astype(jnp.bfloat16)
    gates = jax.nn.sigmoid(jnp.dot(normed, w_gate, preferred_element_type=jnp.float32))
    bias_full = gathered_by_axis(pair_bias, ROWS, 2)
    initial = (
        jnp.full((local_rows, head_count, local_keys), -1e30, jnp.float32),
        jnp.zeros((local_rows, head_count, local_keys), jnp.float32),
        jnp.zeros((local_rows, local_keys, head_count, inner_width // head_count), jnp.float32),
    )
    piece = lax.all_gather(normed, "keys", axis=1, tiled=True)

    def one_block(arrays):
        highest, totals, summed, query_block, input_block = arrays
        key_block = jnp.dot(input_block, w_key, preferred_element_type=jnp.float32).astype(
            jnp.bfloat16
        )
        value_block = jnp.dot(input_block, w_value, preferred_element_type=jnp.float32).astype(
            jnp.bfloat16
        )
        return absorb(
            (highest, totals, summed), query_block, key_block, value_block, bias_full, head_count
        )

    results = lax.map(one_block, tuple((blocked(tensor) for tensor in initial + (queries, piece))))
    highest, totals, summed = tuple((unblocked(tensor) for tensor in results))
    attended = summed / jnp.transpose(totals, (0, 2, 1))[..., None]
    attended = attended.reshape(local_rows, local_keys, inner_width)
    gated = (gates * attended).astype(jnp.bfloat16)
    return jnp.dot(gated, w_out, preferred_element_type=jnp.float32).astype(jnp.bfloat16)


def solution(mesh):
    torus = Mesh(mesh.devices.reshape(4, 4, mesh.shape["keys"]), ("rows_0", "rows_1", "keys"))
    placed = (P(ROWS, "keys", None), P(), P(), P(), P(), P(), P(), P(None, "keys", ROWS))
    return jax.shard_map(
        body, mesh=torus, in_specs=placed, out_specs=P(ROWS, "keys", None), check_vma=False
    )
```

profile of v0, /device:TPU:1, one launch (start us, length us, event | category | flops | bytes accessed | tf_op | source)
XLA Modules:
  0.0 142.0 jit_solution(230207090936119171)
XLA Ops:
  6.6 1.5 %convert_reduce_fusion = f32[48,48]{1,0:T(8,128)S(1)} fusion(bf16[48,48,128]{2,1,0:T(8,128)(2,1)} %param.10), kind=kLoop, calls=%fused_computation.27 | loop fusion | flops 587520 | bytes 599040 | tf_op jit(solution)/shard_map/reduce_sum | solution.py:21
  8.1 1.8 %fusion.35 = f32[48,48]{1,0:T(8,128)S(1)} fusion(bf16[48,48,128]{2,1,0:T(8,128)(2,1)} %param.10, f32[48,48]{1,0:T(8,128)S(1)} %broadcast_multiply_fusion), kind=kLoop, calls=%fused_computation.39 | loop fusion | flops 1177344 | bytes 608256 | tf_op jit(solution)/shard_map/reduce_sum | solution.py:22
  9.9 2.2 %fusion.37 = bf16[48,48,128]{2,1,0:T(8,128)(2,1)} fusion(bf16[48,48,128]{2,1,0:T(8,128)(2,1)S(1)} %copy-done.1, f32[128]{0:T(128)} %param.11, f32[48,48]{1,0:T(8,128)S(1)} %add_rsqrt_fusion, f32[48,48]{1,0:T(8,128)S(1)} %broadcast_multiply_fusion), kind=kLoop, calls=%fused_computation.41 | loop fusion | flops 1474560 | bytes 1198592 | tf_op jit(solution)/shard_map/convert_element_type | solution.py:23
  12.4 10.5 %all_gather.10 = bf16[4,48,192]{1,0,2:T(4,128)(2,1)S(1)} all-gather(bf16[4,48,48]{1,0,2:T(4,128)(2,1)S(1)} %copy.25), channel_id=1, replica_groups=mesh['rows_0'=4,'rows_1'=4,'keys'=16] {'rows_1'}, dimensions={2}, use_global_device_ids=true | all-gather | bytes 92160 | tf_op jit(solution)/shard_map/all_gather | solution.py:15
  22.8 12.1 %all_gather.11 = bf16[4,48,768]{1,0,2:T(4,128)(2,1)S(1)} all-gather(bf16[4,48,192]{1,0,2:T(4,128)(2,1)S(1)} %all_gather.10), channel_id=1, replica_groups=mesh['rows_0'=4,'rows_1'=4,'keys'=16] {'rows_0'}, dimensions={2}, use_global_device_ids=true | all-gather | bytes 368640 | tf_op jit(solution)/shard_map/all_gather | solution.py:15
  35.9 41.3 %all-gather.2.cloned.1.call-done = bf16[48,768,128]{2,1,0:T(8,128)(2,1)} async-done(((bf16[48,48,128]{2,1,0:T(8,128)(2,1)}), bf16[48,768,128]{2,1,0:T(8,128)(2,1)}) %all-gather.2.cloned.1.call-update) | async-done | bytes 9437200 | tf_op jit(solution)/shard_map/all_gather | solution.py:78
  77.2 49.3 %while.12 = (s32[]{:T(128)}, f32[6,8,4,48]{3,2,1,0:T(4,128)S(1)}, f32[6,8,48,4,32]{2,4,3,1,0:T(8,128)}, bf16[6,8,48,128]{3,2,1,0:T(8,128)(2,1)S(1)}, bf16[6,8,76...) while((s32[]{:T(128)}, f32[6,8,4,48]{3,2,1,0:T(4,128)S(1)}, ...), condition=%wide.region_5.6_spmd, body=%wide.region_2.5_spmd.sunk | while | flops 564862464 | bytes 27426936 | solution.py:92
  77.5 2.0 %convolution_convert_fusion.5 = bf16[8,768,128]{1,2,0:T(8,128)(2,1)S(1)} fusion(bf16[6,8,768,128]{3,2,1,0:T(8,128)(2,1)} %get-tuple-element.181, s32[]{:T(128)S(6)} %copy.40, bf16[128,128]{0,1:T(8,128)(2,1)S(1)} %get-tuple-element.182), kind=kOutput, calls=%fused_computation.8.clone.1 | convolution fusion | flops 202113024 | bytes 3178500 | tf_op jit(solution)/shard_map/while/body/eval_jaxpr/dot_general | solution.py:82
  80.5 1.1 fusion.70
  81.6 2.0 %convolution_convert_fusion.6 = bf16[8,768,128]{1,2,0:T(8,128)(2,1)S(1)} fusion(bf16[6,8,768,128]{3,2,1,0:T(8,128)(2,1)} %get-tuple-element.181, s32[]{:T(128)S(6)} %copy.40, bf16[128,128]{0,1:T(8,128)(2,1)S(1)} %get-tuple-element.184), kind=kOutput, calls=%fused_computation.7.clone.1 | convolution fusion | flops 202113024 | bytes 3178500 | tf_op jit(solution)/shard_map/while/body/eval_jaxpr/dot_general | solution.py:85
  83.6 1.9 %fusion.71 = f32[6,8,48,4,32]{2,4,3,1,0:T(8,128)} fusion(f32[6,8,48,4,32]{2,4,3,1,0:T(8,128)} %get-tuple-element.170, s32[]{:T(128)S(6)} %copy.40, bf16[8,768,4,32]{1,3,2,0:T(8,128)(2,1)S(1)} %bitcast.81, f32[8,4,48,768]{3,2,1,0:T(8,128)S(1)} %get-tuple-element.155, f32[8,4,48]{2,1,0:T(4,128)S(1)} %get-tuple-element.157, ...), kind=kOutput, calls=%fused_computation.16.clone.1 | convolution fusion | flops 79085568 | bytes 7417860 | tf_op jit(solution)/shard_map/while/body/eval_jaxpr/rhjk,rkhd->rjhd/dot_general | solution.py:53
  85.7 2.0 %convolution_convert_fusion.5 = bf16[8,768,128]{1,2,0:T(8,128)(2,1)S(1)} fusion(bf16[6,8,768,128]{3,2,1,0:T(8,128)(2,1)} %get-tuple-element.181, s32[]{:T(128)S(6)} %copy.40, bf16[128,128]{0,1:T(8,128)(2,1)S(1)} %get-tuple-element.182), kind=kOutput, calls=%fused_computation.8.clone.1 | convolution fusion | flops 202113024 | bytes 3178500 | tf_op jit(solution)/shard_map/while/body/eval_jaxpr/dot_general | solution.py:82
  88.7 1.1 fusion.70
  89.8 2.0 %convolution_convert_fusion.6 = bf16[8,768,128]{1,2,0:T(8,128)(2,1)S(1)} fusion(bf16[6,8,768,128]{3,2,1,0:T(8,128)(2,1)} %get-tuple-element.181, s32[]{:T(128)S(6)} %copy.40, bf16[128,128]{0,1:T(8,128)(2,1)S(1)} %get-tuple-element.184), kind=kOutput, calls=%fused_computation.7.clone.1 | convolution fusion | flops 202113024 | bytes 3178500 | tf_op jit(solution)/shard_map/while/body/eval_jaxpr/dot_general | solution.py:85
  91.8 1.9 %fusion.71 = f32[6,8,48,4,32]{2,4,3,1,0:T(8,128)} fusion(f32[6,8,48,4,32]{2,4,3,1,0:T(8,128)} %get-tuple-element.170, s32[]{:T(128)S(6)} %copy.40, bf16[8,768,4,32]{1,3,2,0:T(8,128)(2,1)S(1)} %bitcast.81, f32[8,4,48,768]{3,2,1,0:T(8,128)S(1)} %get-tuple-element.155, f32[8,4,48]{2,1,0:T(4,128)S(1)} %get-tuple-element.157, ...), kind=kOutput, calls=%fused_computation.16.clone.1 | convolution fusion | flops 79085568 | bytes 7417860 | tf_op jit(solution)/shard_map/while/body/eval_jaxpr/rhjk,rkhd->rjhd/dot_general | solution.py:53
  93.9 2.0 %convolution_convert_fusion.5 = bf16[8,768,128]{1,2,0:T(8,128)(2,1)S(1)} fusion(bf16[6,8,768,128]{3,2,1,0:T(8,128)(2,1)} %get-tuple-element.181, s32[]{:T(128)S(6)} %copy.40, bf16[128,128]{0,1:T(8,128)(2,1)S(1)} %get-tuple-element.182), kind=kOutput, calls=%fused_computation.8.clone.1 | convolution fusion | flops 202113024 | bytes 3178500 | tf_op jit(solution)/shard_map/while/body/eval_jaxpr/dot_general | solution.py:82
  96.9 1.1 fusion.70
  98.0 2.0 %convolution_convert_fusion.6 = bf16[8,768,128]{1,2,0:T(8,128)(2,1)S(1)} fusion(bf16[6,8,768,128]{3,2,1,0:T(8,128)(2,1)} %get-tuple-element.181, s32[]{:T(128)S(6)} %copy.40, bf16[128,128]{0,1:T(8,128)(2,1)S(1)} %get-tuple-element.184), kind=kOutput, calls=%fused_computation.7.clone.1 | convolution fusion | flops 202113024 | bytes 3178500 | tf_op jit(solution)/shard_map/while/body/eval_jaxpr/dot_general | solution.py:85
  100.0 1.9 %fusion.71 = f32[6,8,48,4,32]{2,4,3,1,0:T(8,128)} fusion(f32[6,8,48,4,32]{2,4,3,1,0:T(8,128)} %get-tuple-element.170, s32[]{:T(128)S(6)} %copy.40, bf16[8,768,4,32]{1,3,2,0:T(8,128)(2,1)S(1)} %bitcast.81, f32[8,4,48,768]{3,2,1,0:T(8,128)S(1)} %get-tuple-element.155, f32[8,4,48]{2,1,0:T(4,128)S(1)} %get-tuple-element.157, ...), kind=kOutput, calls=%fused_computation.16.clone.1 | convolution fusion | flops 79085568 | bytes 7417860 | tf_op jit(solution)/shard_map/while/body/eval_jaxpr/rhjk,rkhd->rjhd/dot_general | solution.py:53
  102.1 2.0 %convolution_convert_fusion.5 = bf16[8,768,128]{1,2,0:T(8,128)(2,1)S(1)} fusion(bf16[6,8,768,128]{3,2,1,0:T(8,128)(2,1)} %get-tuple-element.181, s32[]{:T(128)S(6)} %copy.40, bf16[128,128]{0,1:T(8,128)(2,1)S(1)} %get-tuple-element.182), kind=kOutput, calls=%fused_computation.8.clone.1 | convolution fusion | flops 202113024 | bytes 3178500 | tf_op jit(solution)/shard_map/while/body/eval_jaxpr/dot_general | solution.py:82
  105.2 1.1 fusion.70
  106.2 2.0 %convolution_convert_fusion.6 = bf16[8,768,128]{1,2,0:T(8,128)(2,1)S(1)} fusion(bf16[6,8,768,128]{3,2,1,0:T(8,128)(2,1)} %get-tuple-element.181, s32[]{:T(128)S(6)} %copy.40, bf16[128,128]{0,1:T(8,128)(2,1)S(1)} %get-tuple-element.184), kind=kOutput, calls=%fused_computation.7.clone.1 | convolution fusion | flops 202113024 | bytes 3178500 | tf_op jit(solution)/shard_map/while/body/eval_jaxpr/dot_general | solution.py:85
  108.2 1.9 %fusion.71 = f32[6,8,48,4,32]{2,4,3,1,0:T(8,128)} fusion(f32[6,8,48,4,32]{2,4,3,1,0:T(8,128)} %get-tuple-element.170, s32[]{:T(128)S(6)} %copy.40, bf16[8,768,4,32]{1,3,2,0:T(8,128)(2,1)S(1)} %bitcast.81, f32[8,4,48,768]{3,2,1,0:T(8,128)S(1)} %get-tuple-element.155, f32[8,4,48]{2,1,0:T(4,128)S(1)} %get-tuple-element.157, ...), kind=kOutput, calls=%fused_computation.16.clone.1 | convolution fusion | flops 79085568 | bytes 7417860 | tf_op jit(solution)/shard_map/while/body/eval_jaxpr/rhjk,rkhd->rjhd/dot_general | solution.py:53
  110.4 2.0 %convolution_convert_fusion.5 = bf16[8,768,128]{1,2,0:T(8,128)(2,1)S(1)} fusion(bf16[6,8,768,128]{3,2,1,0:T(8,128)(2,1)} %get-tuple-element.181, s32[]{:T(128)S(6)} %copy.40, bf16[128,128]{0,1:T(8,128)(2,1)S(1)} %get-tuple-element.182), kind=kOutput, calls=%fused_computation.8.clone.1 | convolution fusion | flops 202113024 | bytes 3178500 | tf_op jit(solution)/shard_map/while/body/eval_jaxpr/dot_general | solution.py:82
  114.5 2.0 %convolution_convert_fusion.6 = bf16[8,768,128]{1,2,0:T(8,128)(2,1)S(1)} fusion(bf16[6,8,768,128]{3,2,1,0:T(8,128)(2,1)} %get-tuple-element.181, s32[]{:T(128)S(6)} %copy.40, bf16[128,128]{0,1:T(8,128)(2,1)S(1)} %get-tuple-element.184), kind=kOutput, calls=%fused_computation.7.clone.1 | convolution fusion | flops 202113024 | bytes 3178500 | tf_op jit(solution)/shard_map/while/body/eval_jaxpr/dot_general | solution.py:85
  116.5 1.9 %fusion.71 = f32[6,8,48,4,32]{2,4,3,1,0:T(8,128)} fusion(f32[6,8,48,4,32]{2,4,3,1,0:T(8,128)} %get-tuple-element.170, s32[]{:T(128)S(6)} %copy.40, bf16[8,768,4,32]{1,3,2,0:T(8,128)(2,1)S(1)} %bitcast.81, f32[8,4,48,768]{3,2,1,0:T(8,128)S(1)} %get-tuple-element.155, f32[8,4,48]{2,1,0:T(4,128)S(1)} %get-tuple-element.157, ...), kind=kOutput, calls=%fused_computation.16.clone.1 | convolution fusion | flops 79085568 | bytes 7417860 | tf_op jit(solution)/shard_map/while/body/eval_jaxpr/rhjk,rkhd->rjhd/dot_general | solution.py:53
  118.6 2.0 %convolution_convert_fusion.5 = bf16[8,768,128]{1,2,0:T(8,128)(2,1)S(1)} fusion(bf16[6,8,768,128]{3,2,1,0:T(8,128)(2,1)} %get-tuple-element.181, s32[]{:T(128)S(6)} %copy.40, bf16[128,128]{0,1:T(8,128)(2,1)S(1)} %get-tuple-element.182), kind=kOutput, calls=%fused_computation.8.clone.1 | convolution fusion | flops 202113024 | bytes 3178500 | tf_op jit(solution)/shard_map/while/body/eval_jaxpr/dot_general | solution.py:82
  122.7 2.0 %convolution_convert_fusion.6 = bf16[8,768,128]{1,2,0:T(8,128)(2,1)S(1)} fusion(bf16[6,8,768,128]{3,2,1,0:T(8,128)(2,1)} %get-tuple-element.181, s32[]{:T(128)S(6)} %copy.40, bf16[128,128]{0,1:T(8,128)(2,1)S(1)} %get-tuple-element.184), kind=kOutput, calls=%fused_computation.7.clone.1 | convolution fusion | flops 202113024 | bytes 3178500 | tf_op jit(solution)/shard_map/while/body/eval_jaxpr/dot_general | solution.py:85
  124.7 1.9 %fusion.71 = f32[6,8,48,4,32]{2,4,3,1,0:T(8,128)} fusion(f32[6,8,48,4,32]{2,4,3,1,0:T(8,128)} %get-tuple-element.170, s32[]{:T(128)S(6)} %copy.40, bf16[8,768,4,32]{1,3,2,0:T(8,128)(2,1)S(1)} %bitcast.81, f32[8,4,48,768]{3,2,1,0:T(8,128)S(1)} %get-tuple-element.155, f32[8,4,48]{2,1,0:T(4,128)S(1)} %get-tuple-element.157, ...), kind=kOutput, calls=%fused_computation.16.clone.1 | convolution fusion | flops 79085568 | bytes 7417860 | tf_op jit(solution)/shard_map/while/body/eval_jaxpr/rhjk,rkhd->rjhd/dot_general | solution.py:53
  126.5 3.1 %copy.30 = f32[48,48,128]{2,1,0:T(8,128)} copy(f32[48,48,128]{1,2,0:T(8,128)} %bitcast.85) | data formatting | bytes 2359296 | tf_op jit(solution)/shard_map/reshape | solution.py:35
  129.9 2.0 %copy.31 = f32[48,48,128]{2,1,0:T(8,128)} copy(f32[48,48,128]{1,2,0:T(8,128)S(1)} %bitcast.84) | data formatting | bytes 2359296 | tf_op jit(solution)/shard_map/div | solution.py:94
  131.9 3.3 %convolution_convert_fusion.2 = bf16[48,48,128]{2,1,0:T(8,128)(2,1)} fusion(bf16[48,48,128]{2,1,0:T(8,128)(2,1)} %fusion.37, f32[48,48,128]{2,1,0:T(8,128)} %copy.30, f32[48,48,128]{2,1,0:T(8,128)} %copy.31, bf16[128,128]{1,0:T(8,128)(2,1)S(1)} %copy-done.6, bf16[128,128]{1,0:T(8,128)(2,1)S(1)} %copy-done.7), kind=kOutput, calls=%fused_computation.38 | convolution fusion | flops 153059328 | bytes 3604480 | tf_op jit(solution)/shard_map/dot_general | solution.py:97
  (66 shorter events, 11.2 us)
Async XLA Ops:
  6.5 29.1 %copy-start = (bf16[128,128]{1,0:T(8,128)(2,1)S(1)}, bf16[128,128]{1,0:T(8,128)(2,1)}, u32[]{:S(2)}) copy-start(bf16[128,128]{1,0:T(8,128)(2,1)} %param.12) | copy-start | bytes 98308
  6.5 3.3 %copy-start.1 = (bf16[48,48,128]{2,1,0:T(8,128)(2,1)S(1)}, bf16[48,48,128]{2,1,0:T(8,128)(2,1)}, u32[]{:S(2)}) copy-start(bf16[48,48,128]{2,1,0:T(8,128)(2,1)} %param.10) | copy-start | bytes 1769476
  6.5 5.6 %copy-start.4 = (bf16[128,128]{1,0:T(8,128)(2,1)S(1)}, bf16[128,128]{1,0:T(8,128)(2,1)}, u32[]{:S(2)}) copy-start(bf16[128,128]{1,0:T(8,128)(2,1)} %param.13) | copy-start | bytes 98308
  6.5 5.7 %copy-start.3 = (bf16[4,48,48]{2,1,0:T(8,128)(2,1)S(1)}, bf16[4,48,48]{2,1,0:T(8,128)(2,1)}, u32[]{:S(2)}) copy-start(bf16[4,48,48]{2,1,0:T(8,128)(2,1)} %param.17) | copy-start | bytes 55300
  6.5 70.7 %all-gather.2.cloned.1.call-start = ((), (), s32[]{:S(2)}) async-start(), calls=%async_computation | async-start | bytes 10027008 | tf_op jit(solution)/shard_map/all_gather | solution.py:78
  12.1 23.4 %copy-start.5 = (bf16[128,128]{1,0:T(8,128)(2,1)S(1)}, bf16[128,128]{1,0:T(8,128)(2,1)}, u32[]{:S(2)}) copy-start(bf16[128,128]{1,0:T(8,128)(2,1)} %param.14) | copy-start | bytes 98308
  12.1 23.5 %copy-start.2 = (bf16[48,48,128]{2,1,0:T(8,128)(2,1)S(1)}, bf16[48,48,128]{2,1,0:T(8,128)(2,1)}, u32[]{:S(2)}) copy-start(bf16[48,48,128]{2,1,0:T(8,128)(2,1)} %fusion.37) | copy-start | bytes 1769476
  129.9 2.0 %copy-start.6 = (bf16[128,128]{1,0:T(8,128)(2,1)S(1)}, bf16[128,128]{1,0:T(8,128)(2,1)}, u32[]{:S(2)}) copy-start(bf16[128,128]{1,0:T(8,128)(2,1)} %param.16) | copy-start | bytes 98308
  129.9 2.0 %copy-start.7 = (bf16[128,128]{1,0:T(8,128)(2,1)S(1)}, bf16[128,128]{1,0:T(8,128)(2,1)}, u32[]{:S(2)}) copy-start(bf16[128,128]{1,0:T(8,128)(2,1)} %param.15) | copy-start | bytes 98308
Sparse Core Ops, SparseCore 0:
  12.2 64.9 all-gather.1
where the time goes:
time: 143 us; the launch traced here: 142 us
  matrix products  44.6 us (31%)
  waiting for transfers between devices  41.3 us (29%)
  blocking collectives  22.6 us (16%)
  between operations  13.5 us (9%)
  other arithmetic  12.3 us (9%)
  local copies, waits for them, and re-layouts  7.34 us (5%)
    all_gather x1, waiting for transfers between devices, body(): piece = lax.all_gather(normed, 'keys', axis=1, tiled=True)  41.3 us
    all_gather x2, blocking collectives, gathered_by_axis(): out = lax.all_gather(out, axes[number], axis=dim, tiled=True)  22.6 us
    dot_general x6, matrix products, one_block(): jnp.dot(input_block, w_value, preferred_element_type=jnp.float32)  11.9 us
    dot_general x6, matrix products, one_block(): jnp.dot(input_block, w_key, preferred_element_type=jnp.float32)  11.9 us
    dot_general x6, matrix products, absorb(): jnp.einsum('rhjk,rkhd->rjhd', powers.astype(jnp.bfloat16), split_heads(va...  11.2 us
    reduce_sum x6, other arithmetic, absorb(): totals = totals * shrink + jnp.sum(powers, axis=3)  6.3 us
    dot_general x6, matrix products, absorb(): jnp.einsum('rjhd,rkhd->rhjk', split_heads(query_block, head_count), split...  5.99 us
    dot_general x1, matrix products, body(): jnp.dot(gated, w_out, preferred_element_type=jnp.float32)  3.32 us
  transfers between devices with their start and end apart: 1, of which 1 were waited for; matrix products, arithmetic and copies ran while one was open for 1% of the time, Pallas kernels for 0%

commit v1 on v0

--- a/solution.py
+++ b/solution.py
@@ -75,7 +75,10 @@
         jnp.zeros((local_rows, head_count, local_keys), jnp.float32),
         jnp.zeros((local_rows, local_keys, head_count, inner_width // head_count), jnp.float32),
     )
-    piece = lax.all_gather(normed, "keys", axis=1, tiled=True)
+    devices = lax.axis_size("keys")
+    parts = jnp.stack([normed for _ in range(devices)])
+    parts = lax.all_to_all(parts, "keys", split_axis=0, concat_axis=0)
+    piece = jnp.concatenate(parts, axis=1)
 
     def one_block(arrays):
         highest, totals, summed, query_block, input_block = arrays

time: 143 us -> 295 us (2.06)
  waiting for transfers between devices: 41.3 us -> 182 us
  local copies, waits for them, and re-layouts: 7.34 us -> 22.8 us
  between operations: 13.5 us -> 0.17 us
  starting transfers between devices: 0.03 us -> 10.1 us
    all_to_all x0 -> x1, waiting for transfers between devices: none -> 182 us  [body(): parts = lax.all_to_all(parts, 'keys', split_axis=0, concat_axis=0)]
    all_gather x1 -> x0, waiting for transfers between devices: 41.3 us -> none  [body(): piece = lax.all_gather(normed, 'keys', axis=1, tiled=True)]
    all_to_all x0 -> x1, starting transfers between devices: none -> 10.1 us  [body(): parts = lax.all_to_all(parts, 'keys', split_axis=0, concat_axis=0)]
    all_to_all x0 -> x1, local copies, waits for them, and re-layouts: none -> 10 us  [body(): parts = lax.all_to_all(parts, 'keys', split_axis=0, concat_axis=0)]
    another operation x0 -> x1, local copies, waits for them, and re-layouts: none -> 5.44 us  [body(): parts = jnp.stack([normed for _ in range(devices)])]
  transfers between devices with their start and end apart: 1 -> 1, of which waited for: 1 -> 1; matrix products, arithmetic and copies ran while one was open for 1% -> 0% of each run, Pallas kernels for 0% -> 0%
where the time goes in v1:
time: 295 us; the launch traced here: 294 us
  waiting for transfers between devices  182 us (62%)
  matrix products  44.6 us (15%)
  blocking collectives  23.1 us (8%)
  local copies, waits for them, and re-layouts  22.8 us (8%)
  other arithmetic  11.6 us (4%)
  starting transfers between devices  10.1 us (3%)
    all_to_all x1, waiting for transfers between devices, body(): parts = lax.all_to_all(parts, 'keys', split_axis=0, concat_axis=0)  182 us
    all_gather x2, blocking collectives, gathered_by_axis(): out = lax.all_gather(out, axes[number], axis=dim, tiled=True)  23.1 us
    dot_general x6, matrix products, one_block(): jnp.dot(input_block, w_value, preferred_element_type=jnp.float32)  11.9 us
    dot_general x6, matrix products, one_block(): jnp.dot(input_block, w_key, preferred_element_type=jnp.float32)  11.9 us
    dot_general x6, matrix products, absorb(): jnp.einsum('rhjk,rkhd->rjhd', powers.astype(jnp.bfloat16), split_heads(va...  11.2 us
    all_to_all x1, starting transfers between devices, body(): parts = lax.all_to_all(parts, 'keys', split_axis=0, concat_axis=0)  10.1 us
    all_to_all x1, local copies, waits for them, and re-layouts, body(): parts = lax.all_to_all(parts, 'keys', split_axis=0, concat_axis=0)  10 us
    reduce_sum x6, other arithmetic, absorb(): totals = totals * shrink + jnp.sum(powers, axis=3)  6.3 us
  transfers between devices with their start and end apart: 1, of which 1 were waited for; matrix products, arithmetic and copies ran while one was open for 0% of the time, Pallas kernels for 0%

profile of v1, /device:TPU:1, one launch (start us, length us, event | category | flops | bytes accessed | tf_op | source)
XLA Modules:
  0.0 294.2 jit_solution(1822956246215462606)
XLA Ops:
  0.0 1.5 convert_reduce_fusion
  1.5 1.8 fusion.35
  3.3 1.4 fusion.37
  4.8 5.4 %stack.2 = bf16[16,48,48,128]{3,2,1,0:T(8,128)(2,1)} broadcast(bf16[48,48,128]{2,1,0:T(8,128)(2,1)S(1)} %fusion.37), dimensions={1,2,3} | broadcast | bytes 10027008 | tf_op jit(solution)/shard_map/stack | solution.py:79
  10.2 10.1 %all-to-all-start = ((bf16[16,48,48,128]{3,2,1,0:T(8,128)(2,1)}), bf16[16,48,48,128]{3,2,1,0:T(8,128)(2,1)}, u32[]{:S(2)}, u32[]{:S(2)}) async-start(bf16[16,48,48,128]{3,2,1,0:T(8,128)(2,1)} %stack.2), calls=%async_computation | async-start | bytes 18874368 | tf_op jit(solution)/shard_map/all_to_all | solution.py:80
  20.6 10.4 %all_gather.6 = bf16[4,48,192]{1,0,2:T(4,128)(2,1)S(1)} all-gather(bf16[4,48,48]{1,0,2:T(4,128)(2,1)S(1)} %copy.26), channel_id=1, replica_groups=mesh['rows_0'=4,'rows_1'=4,'keys'=16] {'rows_1'}, dimensions={2}, use_global_device_ids=true | all-gather | bytes 92160 | tf_op jit(solution)/shard_map/all_gather | solution.py:15
  31.0 12.7 %all_gather.7 = bf16[4,48,768]{1,0,2:T(4,128)(2,1)S(1)} all-gather(bf16[4,48,192]{1,0,2:T(4,128)(2,1)S(1)} %all_gather.6), channel_id=1, replica_groups=mesh['rows_0'=4,'rows_1'=4,'keys'=16] {'rows_0'}, dimensions={2}, use_global_device_ids=true | all-gather | bytes 368640 | tf_op jit(solution)/shard_map/all_gather | solution.py:15
  44.6 181.5 %all-to-all-done = bf16[16,48,48,128]{3,2,1,0:T(8,128)(2,1)} async-done(((bf16[16,48,48,128]{3,2,1,0:T(8,128)(2,1)}), bf16[16,48,48,128]{3,2,1,0:T(8,128)(2,1)}, u32[]{:S(2)}, u32[]{:S(2)}) %all-to-all-start) | async-done | bytes 9437216 | tf_op jit(solution)/shard_map/all_to_all | solution.py:80
  226.2 10.0 %copy.25 = bf16[16,48,48,128]{3,2,0,1:T(8,128)(2,1)} copy(bf16[16,48,48,128]{3,2,1,0:T(8,128)(2,1)} %all-to-all-done) | data formatting | bytes 18874368 | tf_op jit(solution)/shard_map/all_to_all | solution.py:80
  236.2 49.3 %while.12 = (s32[]{:T(128)}, f32[6,8,4,48]{3,2,1,0:T(4,128)S(1)}, f32[6,8,48,4,32]{2,4,3,1,0:T(8,128)}, bf16[6,8,48,128]{3,2,1,0:T(8,128)(2,1)S(1)}, bf16[6,8,76...) while((s32[]{:T(128)}, f32[6,8,4,48]{3,2,1,0:T(4,128)S(1)}, ...), condition=%wide.region_5.6_spmd, body=%wide.region_2.5_spmd.sunk | while | flops 564862464 | bytes 27426936 | solution.py:95
  236.4 2.0 convolution_convert_fusion.5
  240.5 2.0 convolution_convert_fusion.6
  242.5 1.9 fusion.71
  244.6 2.0 convolution_convert_fusion.5
  248.8 2.0 convolution_convert_fusion.6
  250.7 1.9 fusion.71
  252.9 2.0 convolution_convert_fusion.5
  255.9 1.1 fusion.70
  257.0 2.0 convolution_convert_fusion.6
  259.0 1.9 fusion.71
  261.1 2.0 convolution_convert_fusion.5
  265.2 2.0 convolution_convert_fusion.6
  267.2 1.9 fusion.71
  269.3 2.0 convolution_convert_fusion.5
  273.4 2.0 convolution_convert_fusion.6
  275.4 1.9 fusion.71
  277.5 2.0 convolution_convert_fusion.5
  281.6 2.0 convolution_convert_fusion.6
  283.6 1.9 fusion.71
  285.5 3.1 %copy.31 = f32[48,48,128]{2,1,0:T(8,128)} copy(f32[48,48,128]{1,2,0:T(8,128)} %bitcast.87) | data formatting | bytes 2359296 | tf_op jit(solution)/shard_map/reshape | solution.py:35
  288.9 2.0 copy.32
  290.9 3.3 %convolution_convert_fusion.2 = bf16[48,48,128]{2,1,0:T(8,128)(2,1)} fusion(bf16[48,48,128]{2,1,0:T(8,128)(2,1)} %copy-done.1, f32[48,48,128]{2,1,0:T(8,128)} %copy.31, f32[48,48,128]{2,1,0:T(8,128)} %copy.32, bf16[128,128]{1,0:T(8,128)(2,1)S(1)} %copy-done.6, bf16[128,128]{1,0:T(8,128)(2,1)S(1)} %copy-done.7), kind=kOutput, calls=%fused_computation.38 | convolution fusion | flops 153059328 | bytes 3604480 | tf_op jit(solution)/shard_map/dot_general | solution.py:100
  (67 shorter events, 14.3 us)
Async XLA Ops:
  0.0 44.3 %copy-start = (bf16[128,128]{1,0:T(8,128)(2,1)S(1)}, bf16[128,128]{1,0:T(8,128)(2,1)}, u32[]{:S(2)}) copy-start(bf16[128,128]{1,0:T(8,128)(2,1)} %param.12) | copy-start | bytes 98308
  0.0 3.3 %copy-start.2 = (bf16[48,48,128]{2,1,0:T(8,128)(2,1)S(1)}, bf16[48,48,128]{2,1,0:T(8,128)(2,1)}, u32[]{:S(2)}) copy-start(bf16[48,48,128]{2,1,0:T(8,128)(2,1)} %param.10) | copy-start | bytes 1769476
  4.8 39.5 %copy-start.1 = (bf16[48,48,128]{2,1,0:T(8,128)(2,1)}, bf16[48,48,128]{2,1,0:T(8,128)(2,1)S(1)}, u32[]{:S(2)}) copy-start(bf16[48,48,128]{2,1,0:T(8,128)(2,1)S(1)} %fusion.37) | copy-start | bytes 1769476
  10.2 10.1 %copy-start.4 = (bf16[128,128]{1,0:T(8,128)(2,1)S(1)}, bf16[128,128]{1,0:T(8,128)(2,1)}, u32[]{:S(2)}) copy-start(bf16[128,128]{1,0:T(8,128)(2,1)} %param.13) | copy-start | bytes 98308
  10.2 10.3 %copy-start.3 = (bf16[4,48,48]{2,1,0:T(8,128)(2,1)S(1)}, bf16[4,48,48]{2,1,0:T(8,128)(2,1)}, u32[]{:S(2)}) copy-start(bf16[4,48,48]{2,1,0:T(8,128)(2,1)} %param.17) | copy-start | bytes 55300
  10.2 215.9 %all-to-all-start = ((bf16[16,48,48,128]{3,2,1,0:T(8,128)(2,1)}), bf16[16,48,48,128]{3,2,1,0:T(8,128)(2,1)}, u32[]{:S(2)}, u32[]{:S(2)}) async-start(bf16[16,48,48,128]{3,2,1,0:T(8,128)(2,1)} %stack.2), calls=%async_computation | async-start | bytes 18874368 | tf_op jit(solution)/shard_map/all_to_all | solution.py:80
  20.3 23.9 %copy-start.5 = (bf16[128,128]{1,0:T(8,128)(2,1)S(1)}, bf16[128,128]{1,0:T(8,128)(2,1)}, u32[]{:S(2)}) copy-start(bf16[128,128]{1,0:T(8,128)(2,1)} %param.14) | copy-start | bytes 98308
  288.9 2.0 copy-start.6
  288.9 2.0 copy-start.7
